TPU v7x, 32 devices: a whole 2x2x4 slice. The times are simulated.
32 devices in a mesh: fsdp: 4 (over z), ctx: 2 (over x), tp: 4 (over y, core).
Axes of the slice: x: 2, y: 2, z: 4, core: 2. Of those that a mesh axis runs over, the one named last changes fastest.
Arguments:
- tokens: bfloat16 [8, 1024, 1024], P('fsdp', ('ctx', 'tp')), may hold values from -6 to 6
- key_valid: int32 [8, 1024], P('fsdp'), may hold values from 0 to 1, as said below
- first_gain: bfloat16 [2, 1024], P(None, 'fsdp'), may hold values from 0.25 to 1.75
- first_shift: bfloat16 [2, 1024], P(None, 'fsdp'), may hold values from -1.75 to 1.75
- joint_weight: bfloat16 [2, 1024, 3, 1024], P(None, 'fsdp', None, 'tp'), may hold values from -0.1875 to 0.1875
- query_bias: bfloat16 [2, 16, 64], P(None, 'tp', 'fsdp'), may hold values from -3 to 3
- value_bias: bfloat16 [2, 16, 64], P(None, 'tp', 'fsdp'), may hold values from -0.625 to 0.625
- out_weight: bfloat16 [2, 1024, 1024], P(None, 'tp', 'fsdp'), may hold values from -0.75 to 0.75
- out_bias: bfloat16 [2, 1024], P(None, 'fsdp'), may hold values from -1.75 to 1.75
- second_gain: bfloat16 [2, 1024], P(None, 'fsdp'), may hold values from 0.25 to 1.75
- second_shift: bfloat16 [2, 1024], P(None, 'fsdp'), may hold values from -1.75 to 1.75
- expand_weight: bfloat16 [2, 1024, 4096], P(None, 'fsdp', 'tp'), may hold values from -0.1875 to 0.1875
- expand_bias: bfloat16 [2, 64, 64], P(None, 'tp', 'fsdp'), may hold values from -3 to 3
- reduce_weight: bfloat16 [2, 4096, 1024], P(None, 'tp', 'fsdp'), may hold values from -0.09375 to 0.09375
- reduce_bias: bfloat16 [2, 1024], P(None, 'fsdp'), may hold values from -1.75 to 1.75
- cotangent: bfloat16 [8, 1024, 1024], P('fsdp', ('ctx', 'tp')), may hold values from -6 to 6
Outputs:
- output: bfloat16 [8, 1024, 1024], P('fsdp', ('ctx', 'tp'))
- input_grad: bfloat16 [8, 1024, 1024], P('fsdp', ('ctx', 'tp'))
- grad_first_gain: float32 [2, 1024], P(None, 'fsdp')
- grad_first_shift: float32 [2, 1024], P(None, 'fsdp')
- grad_joint_weight: float32 [2, 1024, 3, 1024], P(None, 'fsdp', None, 'tp')
- grad_query_bias: float32 [2, 16, 64], P(None, 'tp', 'fsdp')
- grad_value_bias: float32 [2, 16, 64], P(None, 'tp', 'fsdp')
- grad_out_weight: float32 [2, 1024, 1024], P(None, 'tp', 'fsdp')
- grad_out_bias: float32 [2, 1024], P(None, 'fsdp')
- grad_second_gain: float32 [2, 1024], P(None, 'fsdp')
- grad_second_shift: float32 [2, 1024], P(None, 'fsdp')
- grad_expand_weight: float32 [2, 1024, 4096], P(None, 'fsdp', 'tp')
- grad_expand_bias: float32 [2, 64, 64], P(None, 'tp', 'fsdp')
- grad_reduce_weight: float32 [2, 4096, 1024], P(None, 'tp', 'fsdp')
- grad_reduce_bias: float32 [2, 1024], P(None, 'fsdp')
Inputs may be any that keep to these rules, and one draw needn't show every extreme that they name: `key_valid`: in each clip the ones form a prefix of 128 tokens or more; clip 0 has ones throughout.
All inputs are finite; a program needn't handle non-finite values.
Results may differ from a plain program's by a relative error of at most 0.02.
Values may be sent and summed in bfloat16 or wider, within the bound.
A program may use at most 256 MiB of HBM per device.

v0:
```python
import jax
import jax.numpy as jnp
from jax import lax
from jax.sharding import PartitionSpec as P

HD = 64
LAYERS = 2
MB = 2
epsilon = 1e-06
masked_score = -10000.0


def norm_rows(rows, gain, shift):
    middle = jnp.mean(rows, axis=-1, keepdims=True)
    centred = rows - middle
    spread = jnp.mean(centred * centred, axis=-1, keepdims=True)
    return centred * lax.rsqrt(spread + epsilon) * gain + shift


def exact_gelu(values):
    return jax.nn.gelu(values, approximate=False)


def dense(left, right):
    return jnp.dot(left, right, preferred_element_type=jnp.float32)


def dense_left(left, right):
    return lax.dot_general(
        left, right, (((0,), (0,)), ((), ())), preferred_element_type=jnp.float32
    )


def dense_right(left, right):
    return lax.dot_general(
        left, right, (((1,), (1,)), ((), ())), preferred_element_type=jnp.float32
    )


def head_major(rows):
    return rows.reshape(rows.shape[0], -1, HD).transpose(1, 0, 2)


def row_major(heads):
    return heads.transpose(1, 0, 2).reshape(heads.shape[1], -1)


def spread_rows(rows):
    return lax.all_gather(rows, "tp", axis=0, tiled=True)


def gather_grad(rows):
    return lax.all_gather(rows, "tp", axis=0, tiled=True)


def combine_rows(partial_value):
    return lax.psum_scatter(
        partial_value.astype(jnp.bfloat16), "tp", scatter_dimension=0, tiled=True
    ).astype(jnp.float32)


def combine_grads(partial_value):
    return lax.psum_scatter(
        partial_value.astype(jnp.bfloat16), "tp", scatter_dimension=0, tiled=True
    ).astype(jnp.float32)


def fetch(params, layer_id):
    (
        first_gain,
        first_shift,
        joint_weight,
        query_bias,
        value_bias,
        out_weight,
        out_bias,
        second_gain,
        second_shift,
        expand_weight,
        expand_bias,
        reduce_weight,
        reduce_bias,
    ) = params
    return (
        lax.all_gather(first_gain[layer_id], "fsdp", axis=0, tiled=True),
        lax.all_gather(first_shift[layer_id], "fsdp", axis=0, tiled=True),
        lax.all_gather(joint_weight[layer_id], "fsdp", axis=0, tiled=True),
        lax.all_gather(query_bias[layer_id], "fsdp", axis=1, tiled=True),
        lax.all_gather(value_bias[layer_id], "fsdp", axis=1, tiled=True),
        lax.all_gather(out_weight[layer_id], "fsdp", axis=1, tiled=True),
        lax.all_gather(out_bias[layer_id], "fsdp", axis=0, tiled=True),
        lax.all_gather(second_gain[layer_id], "fsdp", axis=0, tiled=True),
        lax.all_gather(second_shift[layer_id], "fsdp", axis=0, tiled=True),
        lax.all_gather(expand_weight[layer_id], "fsdp", axis=0, tiled=True),
        lax.all_gather(expand_bias[layer_id], "fsdp", axis=1, tiled=True),
        lax.all_gather(reduce_weight[layer_id], "fsdp", axis=1, tiled=True),
        lax.all_gather(reduce_bias[layer_id], "fsdp", axis=0, tiled=True),
    )


def attention_scores(query_heads, key_heads, key_bias):
    raw_scores = jnp.einsum(
        "hqd,hkd->hqk", query_heads, key_heads, preferred_element_type=jnp.float32
    )
    return raw_scores * HD ** (-0.5) + key_bias


def forward_layer(residual, layer_weights, key_bias):
    (
        gain_attn,
        shift_attn,
        joint_mat,
        query_add,
        value_add,
        out_mat,
        out_add,
        gain_mlp,
        shift_mlp,
        expand_mat,
        expand_add,
        reduce_mat,
        reduce_add,
    ) = layer_weights
    normed = norm_rows(residual, gain_attn.astype(jnp.float32), shift_attn.astype(jnp.float32))
    first_in = spread_rows(normed.astype(jnp.bfloat16))
    joint = jnp.einsum("nd,dce->nce", first_in, joint_mat, preferred_element_type=jnp.float32)
    queries = (joint[:, 0] + query_add.reshape(-1).astype(jnp.float32)).astype(jnp.bfloat16)
    keys_local = joint[:, 1].astype(jnp.bfloat16)
    values_local = (joint[:, 2] + value_add.reshape(-1).astype(jnp.float32)).astype(jnp.bfloat16)
    keys_all, values_all = (
        lax.all_gather(keys_local, "ctx", axis=0, tiled=True),
        lax.all_gather(values_local, "ctx", axis=0, tiled=True),
    )
    query_heads = head_major(queries)
    key_heads = head_major(keys_all)
    value_heads = head_major(values_all)
    scores = attention_scores(query_heads, key_heads, key_bias)
    row_top = jnp.max(scores, axis=-1, keepdims=True)
    exponent = jnp.exp(scores - row_top)
    row_total = jnp.sum(exponent, axis=-1, keepdims=True)
    probs_low = (exponent / row_total).astype(jnp.bfloat16)
    log_total = row_top + jnp.log(row_total)
    mixed_heads = jnp.einsum(
        "hqk,hkd->hqd", probs_low, value_heads, preferred_element_type=jnp.float32
    )
    mixed = row_major(mixed_heads.astype(jnp.bfloat16))
    middle = residual + (combine_rows(dense(mixed, out_mat)) + out_add.astype(jnp.float32))
    normed_mlp = norm_rows(middle, gain_mlp.astype(jnp.float32), shift_mlp.astype(jnp.float32))
    second_in = spread_rows(normed_mlp.astype(jnp.bfloat16))
    before = dense(second_in, expand_mat) + expand_add.reshape(-1).astype(jnp.float32)
    active = exact_gelu(before).astype(jnp.bfloat16)
    result = middle + (combine_rows(dense(active, reduce_mat)) + reduce_add.astype(jnp.float32))
    stored = (
        residual,
        first_in,
        query_heads,
        key_heads,
        value_heads,
        log_total,
        mixed,
        middle,
        second_in,
        before,
        active,
    )
    return (result, stored)


def backward_layer(carry, stored, layer_weights, key_bias):
    (
        gain_attn,
        shift_attn,
        joint_mat,
        query_add,
        value_add,
        out_mat,
        out_add,
        gain_mlp,
        shift_mlp,
        expand_mat,
        expand_add,
        reduce_mat,
        reduce_add,
    ) = layer_weights
    (
        residual,
        first_in,
        query_heads,
        key_heads,
        value_heads,
        log_total,
        mixed,
        middle,
        second_in,
        before,
        active,
    ) = stored
    low_mlp = carry.astype(jnp.bfloat16)
    mlp_rows = gather_grad(low_mlp)
    d_reduce_mat = dense_left(active, mlp_rows)
    d_reduce_add = jnp.sum(low_mlp.astype(jnp.float32), axis=0)
    d_active = dense_right(mlp_rows, reduce_mat)
    gelu_value, gelu_back = jax.vjp(exact_gelu, before)
    d_before = gelu_back(d_active)[0].astype(jnp.bfloat16)
    d_expand_add = jnp.sum(d_before.astype(jnp.float32), axis=0).reshape(expand_add.shape)
    d_expand_mat = dense_left(second_in, d_before)
    d_second = combine_grads(dense_right(d_before, expand_mat))
    norm_value, norm_back = jax.vjp(
        norm_rows, middle, gain_mlp.astype(jnp.float32), shift_mlp.astype(jnp.float32)
    )
    d_middle, d_gain_mlp, d_shift_mlp = norm_back(d_second)
    carry_mid = carry + d_middle
    low_attn = carry_mid.astype(jnp.bfloat16)
    attn_rows = gather_grad(low_attn)
    d_out_mat = dense_left(mixed, attn_rows)
    d_out_add = jnp.sum(low_attn.astype(jnp.float32), axis=0)
    d_mixed = head_major(dense_right(attn_rows, out_mat).astype(jnp.bfloat16))
    scores = attention_scores(query_heads, key_heads, key_bias)
    attn_probs = jnp.exp(scores - log_total)
    d_values = jnp.einsum(
        "hqk,hqd->hkd", attn_probs.astype(jnp.bfloat16), d_mixed, preferred_element_type=jnp.float32
    )
    d_probs = jnp.einsum("hqd,hkd->hqk", d_mixed, value_heads, preferred_element_type=jnp.float32)
    d_scores = attn_probs * (d_probs - jnp.sum(attn_probs * d_probs, axis=-1, keepdims=True))
    d_raw = (d_scores * HD ** (-0.5)).astype(jnp.bfloat16)
    d_queries = jnp.einsum("hqk,hkd->hqd", d_raw, key_heads, preferred_element_type=jnp.float32)
    d_queries = row_major(d_queries.astype(jnp.bfloat16))
    d_keys = jnp.einsum("hqk,hqd->hkd", d_raw, query_heads, preferred_element_type=jnp.float32)
    d_keys = row_major(d_keys)
    d_values = row_major(d_values)
    d_keys, d_values = (
        lax.psum_scatter(
            d_keys.astype(jnp.bfloat16), "ctx", scatter_dimension=0, tiled=True
        ).astype(jnp.float32),
        lax.psum_scatter(
            d_values.astype(jnp.bfloat16), "ctx", scatter_dimension=0, tiled=True
        ).astype(jnp.float32),
    )
    d_keys = d_keys.astype(jnp.bfloat16)
    d_values = d_values.astype(jnp.bfloat16)
    d_joint = jnp.stack((d_queries, d_keys, d_values), axis=1)
    d_joint_mat = jnp.einsum("nd,nce->dce", first_in, d_joint, preferred_element_type=jnp.float32)
    d_query_add = jnp.sum(d_queries.astype(jnp.float32), axis=0).reshape(query_add.shape)
    d_value_add = jnp.sum(d_values.astype(jnp.float32), axis=0).reshape(value_add.shape)
    d_first = combine_grads(
        jnp.einsum("nce,dce->nd", d_joint, joint_mat, preferred_element_type=jnp.float32)
    )
    first_value, first_back = jax.vjp(
        norm_rows, residual, gain_attn.astype(jnp.float32), shift_attn.astype(jnp.float32)
    )
    d_residual, d_gain_attn, d_shift_attn = first_back(d_first)
    carry_in = carry_mid + d_residual
    layer_grads = (
        d_gain_attn,
        d_shift_attn,
        d_joint_mat,
        d_query_add,
        d_value_add,
        d_out_mat,
        d_out_add,
        d_gain_mlp,
        d_shift_mlp,
        d_expand_mat,
        d_expand_add,
        d_reduce_mat,
        d_reduce_add,
    )
    return (carry_in, layer_grads)


def local(
    tokens,
    key_valid,
    first_gain,
    first_shift,
    joint_weight,
    query_bias,
    value_bias,
    out_weight,
    out_bias,
    second_gain,
    second_shift,
    expand_weight,
    expand_bias,
    reduce_weight,
    reduce_bias,
    cotangent,
):
    params = (
        first_gain,
        first_shift,
        joint_weight,
        query_bias,
        value_bias,
        out_weight,
        out_bias,
        second_gain,
        second_shift,
        expand_weight,
        expand_bias,
        reduce_weight,
        reduce_bias,
    )
    fetched = tuple((fetch(params, layer_id) for layer_id in range(LAYERS)))
    totals = [None] * LAYERS
    outputs = []
    row_grads = []
    for batch_id in range(MB):
        key_bias = jnp.where(key_valid[batch_id] == 1, 0.0, masked_score).astype(jnp.float32)
        residual = tokens[batch_id].astype(jnp.float32)
        stores = []
        for layer_id in range(LAYERS):
            residual, stored = forward_layer(residual, fetched[layer_id], key_bias)
            stores.append(stored)
        outputs.append(residual.astype(jnp.bfloat16))
        carry = cotangent[batch_id].astype(jnp.float32)
        for layer_id in reversed(range(LAYERS)):
            carry, layer_grads = backward_layer(
                carry, stores[layer_id], fetched[layer_id], key_bias
            )
            if totals[layer_id] is None:
                totals[layer_id] = layer_grads
            else:
                totals[layer_id] = tuple(
                    (old + new for old, new in zip(totals[layer_id], layer_grads))
                )
        row_grads.append(carry.astype(jnp.bfloat16))
    stacked = [
        jnp.stack([totals[layer_id][index] for layer_id in range(LAYERS)]) for index in range(13)
    ]
    shards = (
        lax.psum_scatter(
            stacked[0].astype(jnp.bfloat16), "fsdp", scatter_dimension=1, tiled=True
        ).astype(jnp.float32),
        lax.psum_scatter(
            stacked[1].astype(jnp.bfloat16), "fsdp", scatter_dimension=1, tiled=True
        ).astype(jnp.float32),
        lax.psum_scatter(
            stacked[2].astype(jnp.bfloat16), "fsdp", scatter_dimension=1, tiled=True
        ).astype(jnp.float32),
        lax.psum_scatter(
            stacked[3].astype(jnp.bfloat16), "fsdp", scatter_dimension=2, tiled=True
        ).astype(jnp.float32),
        lax.psum_scatter(
            stacked[4].astype(jnp.bfloat16), "fsdp", scatter_dimension=2, tiled=True
        ).astype(jnp.float32),
        lax.psum_scatter(
            stacked[5].astype(jnp.bfloat16), "fsdp", scatter_dimension=2, tiled=True
        ).astype(jnp.float32),
        lax.psum_scatter(
            stacked[6].astype(jnp.bfloat16), "fsdp", scatter_dimension=1, tiled=True
        ).astype(jnp.float32),
        lax.psum_scatter(
            stacked[7].astype(jnp.bfloat16), "fsdp", scatter_dimension=1, tiled=True
        ).astype(jnp.float32),
        lax.psum_scatter(
            stacked[8].astype(jnp.bfloat16), "fsdp", scatter_dimension=1, tiled=True
        ).astype(jnp.float32),
        lax.psum_scatter(
            stacked[9].astype(jnp.bfloat16), "fsdp", scatter_dimension=1, tiled=True
        ).astype(jnp.float32),
        lax.psum_scatter(
            stacked[10].astype(jnp.bfloat16), "fsdp", scatter_dimension=2, tiled=True
        ).astype(jnp.float32),
        lax.psum_scatter(
            stacked[11].astype(jnp.bfloat16), "fsdp", scatter_dimension=2, tiled=True
        ).astype(jnp.float32),
        lax.psum_scatter(
            stacked[12].astype(jnp.bfloat16), "fsdp", scatter_dimension=1, tiled=True
        ).astype(jnp.float32),
    )
    split_sums = (
        lax.psum(shards[2].astype(jnp.bfloat16), "ctx").astype(jnp.float32),
        lax.psum(shards[3].astype(jnp.bfloat16), "ctx").astype(jnp.float32),
        lax.psum(shards[4].astype(jnp.bfloat16), "ctx").astype(jnp.float32),
        lax.psum(shards[5].astype(jnp.bfloat16), "ctx").astype(jnp.float32),
        lax.psum(shards[9].astype(jnp.bfloat16), "ctx").astype(jnp.float32),
        lax.psum(shards[10].astype(jnp.bfloat16), "ctx").astype(jnp.float32),
        lax.psum(shards[11].astype(jnp.bfloat16), "ctx").astype(jnp.float32),
    )
    vector_part = lax.psum(
        (shards[0], shards[1], shards[6], shards[7], shards[8], shards[12]), ("ctx", "tp")
    )
    return (
        jnp.stack(outputs),
        jnp.stack(row_grads),
        vector_part[0],
        vector_part[1],
        split_sums[0],
        split_sums[1],
        split_sums[2],
        split_sums[3],
        vector_part[2],
        vector_part[3],
        vector_part[4],
        split_sums[4],
        split_sums[5],
        split_sums[6],
        vector_part[5],
    )


def solution(mesh):
    placed = (
        P("fsdp", ("ctx", "tp"), None),
        P("fsdp", None),
        P(None, "fsdp"),
        P(None, "fsdp"),
        P(None, "fsdp", None, "tp"),
        P(None, "tp", "fsdp"),
        P(None, "tp", "fsdp"),
        P(None, "tp", "fsdp"),
        P(None, "fsdp"),
        P(None, "fsdp"),
        P(None, "fsdp"),
        P(None, "fsdp", "tp"),
        P(None, "tp", "fsdp"),
        P(None, "tp", "fsdp"),
        P(None, "fsdp"),
        P("fsdp", ("ctx", "tp"), None),
    )
    return jax.shard_map(
        local,
        mesh=mesh,
        in_specs=placed,
        out_specs=(
            P("fsdp", ("ctx", "tp"), None),
            P("fsdp", ("ctx", "tp"), None),
            P(None, "fsdp"),
            P(None, "fsdp"),
            P(None, "fsdp", None, "tp"),
            P(None, "tp", "fsdp"),
            P(None, "tp", "fsdp"),
            P(None, "tp", "fsdp"),
            P(None, "fsdp"),
            P(None, "fsdp"),
            P(None, "fsdp"),
            P(None, "fsdp", "tp"),
            P(None, "tp", "fsdp"),
            P(None, "tp", "fsdp"),
            P(None, "fsdp"),
        ),
        check_vma=False,
    )
```

profile of v0, /device:TPU:0, one launch (start us, length us, event | category | flops | bytes accessed | tf_op | source)
XLA Modules:
  0.0 1841.4 jit_solution(5257562722936392963)
XLA Ops:
  240.8 27.9 %all-gather.85.cloned.1.call-done = bf16[1,1024,1024]{2,1,0:T(8,128)(2,1)} async-done(((bf16[1,256,1024]{2,1,0:T(8,128)(2,1)}), bf16[1,1024,1024]{2,1,0:T(8,128)(2,1)}) %all-gather.85.cloned.1.call-update) | async-done | bytes 2097168 | tf_op jit(solution)/shard_map/all_gather | solution.py:94
  318.6 35.0 %all-gather.87.cloned.1.call-done = bf16[1,1024,1024]{2,1,0:T(8,128)(2,1)} async-done(((bf16[1,1024,256]{2,1,0:T(8,128)(2,1)}), bf16[1,1024,1024]{2,1,0:T(8,128)(2,1)}) %all-gather.87.cloned.1.call-update) | async-done | bytes 2097168 | tf_op jit(solution)/shard_map/all_gather | solution.py:96
  388.2 20.1 %reduce-scatter.66.cloned.1.call-done = bf16[128,1024]{1,0:T(8,128)(2,1)} async-done(((bf16[512,1024]{1,0:T(8,128)(2,1)}), bf16[128,1024]{1,0:T(8,128)(2,1)}) %reduce-scatter.66.cloned.1.call-update) | async-done | bytes 262160 | tf_op jit(solution)/shard_map/reduce_scatter | solution.py:57
  597.3 27.3 %all-gather.91.cloned.1.call-done = bf16[1,1024,1024]{2,1,0:T(8,128)(2,1)} async-done(((bf16[1,256,1024]{2,1,0:T(8,128)(2,1)}), bf16[1,1024,1024]{2,1,0:T(8,128)(2,1)}) %all-gather.91.cloned.1.call-update) | async-done | bytes 2097168 | tf_op jit(solution)/shard_map/all_gather | solution.py:94
  678.8 48.4 %all-gather.93.cloned.1.call-done = bf16[1,1024,1024]{2,1,0:T(8,128)(2,1)} async-done(((bf16[1,1024,256]{2,1,0:T(8,128)(2,1)}), bf16[1,1024,1024]{2,1,0:T(8,128)(2,1)}) %all-gather.93.cloned.1.call-update) | async-done | bytes 2097168 | tf_op jit(solution)/shard_map/all_gather | solution.py:96
  771.9 26.8 %reduce-scatter.72.cloned.1.call-done = bf16[128,1024]{1,0:T(8,128)(2,1)} async-done(((bf16[512,1024]{1,0:T(8,128)(2,1)}), bf16[128,1024]{1,0:T(8,128)(2,1)}) %reduce-scatter.72.cloned.1.call-update) | async-done | bytes 262160 | tf_op jit(solution)/shard_map/reduce_scatter | solution.py:63
  800.1 26.0 %reduce-scatter.62.cloned.1.call-done = bf16[128,1024]{1,0:T(8,128)(2,1)} async-done(((bf16[512,1024]{1,0:T(8,128)(2,1)}), bf16[128,1024]{1,0:T(8,128)(2,1)}) %reduce-scatter.62.cloned.1.call-update) | async-done | bytes 262160 | tf_op jit(solution)/shard_map/reduce_scatter | solution.py:57
  826.1 27.5 %reduce-scatter.70.cloned.1.call-done = bf16[128,1024]{1,0:T(8,128)(2,1)} async-done(((bf16[512,1024]{1,0:T(8,128)(2,1)}), bf16[128,1024]{1,0:T(8,128)(2,1)}) %reduce-scatter.70.cloned.1.call-update) | async-done | bytes 262160 | tf_op jit(solution)/shard_map/reduce_scatter | solution.py:57
  881.5 23.0 %fusion.221 = bf16[4,1024,64]{1,2,0:T(8,128)(2,1)} fusion(f32[4,512,1024]{2,1,0:T(8,128)} %fusion.467, f32[4,512,1024]{2,1,0:T(8,128)} %copy-done.4, f32[4,512]{1,0:T(4,128)S(1)} %log_add_fusion.1, f32[1024]{0:T(1024)S(1)} %bitcast.661, f32[512,4,64]{0,2,1:T(8,128)S(1)} %bitcast.579, f32[4,64]{1,0:T(4,128)S(1)} %copy.126), kind=kOutput, calls=%fused_computation.234 | convolution fusion | flops 292031488 | bytes 17839104 | tf_op jit(solution)/shard_map/hqk,hqd->hkd/dot_general | solution.py:228
  921.5 22.2 %fusion.227 = bf16[4,1024,64]{1,2,0:T(8,128)(2,1)S(1)} fusion(f32[4,512,1024]{2,1,0:T(8,128)} %fusion.465, f32[4,512,1024]{2,1,0:T(8,128)} %copy-done.3, f32[4,512]{1,0:T(4,128)S(1)} %log_add_fusion.3, f32[1024]{0:T(1024)S(1)} %bitcast.649, f32[512,4,64]{0,2,1:T(8,128)S(1)} %bitcast.577, f32[4,64]{1,0:T(4,128)S(1)} %copy.126), kind=kOutput, calls=%fused_computation.236 | convolution fusion | flops 292031488 | bytes 17839104 | tf_op jit(solution)/shard_map/hqk,hqd->hkd/dot_general | solution.py:228
  951.3 21.7 %convert_reduce_fusion.26 = (f32[4,64]{1,0:T(4,128)S(1)}, bf16[4,512,64]{1,2,0:T(8,128)(2,1)S(1)}) fusion(bf16[4,1024,64]{1,2,0:T(8,128)(2,1)S(1)} %bitcast.575, f32[4,512,1024]{2,1,0:T(8,128)} %fusion.467, f32[4,512,1024]{2,1,0:T(8,128)} %copy-done.4, f32[4,512]{1,0:T(4,128)S(1)} %log_add_fusion.1, f32[1024]{0:T(1024)S(1)} %bitcast.663), kind=kOutput, calls=%fused_computation.405 | convolution fusion | flops 291900160 | bytes 17576960 | tf_op jit(solution)/shard_map/hqk,hkd->hqd/dot_general | solution.py:226
  977.0 21.7 %convert_reduce_fusion.27 = (f32[4,64]{1,0:T(4,128)S(1)}, bf16[4,512,64]{1,2,0:T(8,128)(2,1)S(1)}) fusion(bf16[4,1024,64]{1,2,0:T(8,128)(2,1)S(1)} %bitcast.573, f32[4,512,1024]{2,1,0:T(8,128)} %fusion.465, f32[4,512,1024]{2,1,0:T(8,128)} %copy-done.3, f32[4,512]{1,0:T(4,128)S(1)} %log_add_fusion.3, f32[1024]{0:T(1024)S(1)} %bitcast.651), kind=kOutput, calls=%fused_computation.406 | convolution fusion | flops 291900160 | bytes 17576960 | tf_op jit(solution)/shard_map/hqk,hkd->hqd/dot_general | solution.py:226
  1004.4 27.6 %reduce-scatter.78.cloned.1.call-done = bf16[128,1024]{1,0:T(8,128)(2,1)} async-done(((bf16[512,1024]{1,0:T(8,128)(2,1)}), bf16[128,1024]{1,0:T(8,128)(2,1)}) %reduce-scatter.78.cloned.1.call-update) | async-done | bytes 262160 | tf_op jit(solution)/shard_map/reduce_scatter | solution.py:63
  1099.8 28.2 %reduce-scatter.80.cloned.1.call-done = bf16[128,1024]{1,0:T(8,128)(2,1)} async-done(((bf16[512,1024]{1,0:T(8,128)(2,1)}), bf16[128,1024]{1,0:T(8,128)(2,1)}) %reduce-scatter.80.cloned.1.call-update) | async-done | bytes 262160 | tf_op jit(solution)/shard_map/reduce_scatter | solution.py:63
  1157.4 22.8 %fusion.218 = bf16[4,1024,64]{1,2,0:T(8,128)(2,1)} fusion(f32[4,512,1024]{2,1,0:T(8,128)} %fusion.468, f32[4,512,1024]{2,1,0:T(8,128)} %copy-done.2, f32[4,512]{1,0:T(4,128)S(1)} %log_add_fusion, f32[1024]{0:T(1024)S(1)} %bitcast.664, f32[512,4,64]{0,2,1:T(8,128)S(1)} %bitcast.569, f32[4,64]{1,0:T(4,128)S(1)} %copy-done.104), kind=kOutput, calls=%fused_computation.233 | convolution fusion | flops 292031488 | bytes 17839104 | tf_op jit(solution)/shard_map/hqk,hqd->hkd/dot_general | solution.py:228
  1196.9 22.0 %fusion.224 = bf16[4,1024,64]{1,2,0:T(8,128)(2,1)S(1)} fusion(f32[4,512,1024]{2,1,0:T(8,128)} %fusion.466, f32[4,512,1024]{2,1,0:T(8,128)} %copy-done.1, f32[4,512]{1,0:T(4,128)S(1)} %log_add_fusion.2, f32[1024]{0:T(1024)S(1)} %bitcast.652, f32[512,4,64]{0,2,1:T(8,128)S(1)} %bitcast.563, f32[4,64]{1,0:T(4,128)S(1)} %copy-done.104), kind=kOutput, calls=%fused_computation.235 | convolution fusion | flops 292031488 | bytes 17839104 | tf_op jit(solution)/shard_map/hqk,hqd->hkd/dot_general | solution.py:228
  1226.5 22.1 %convert_reduce_fusion.28 = (f32[4,64]{1,0:T(4,128)}, bf16[4,512,64]{1,2,0:T(8,128)(2,1)S(1)}) fusion(bf16[4,1024,64]{1,2,0:T(8,128)(2,1)S(1)} %bitcast.567, f32[4,512,1024]{2,1,0:T(8,128)} %fusion.468, f32[4,512,1024]{2,1,0:T(8,128)} %copy-done.2, f32[4,512]{1,0:T(4,128)S(1)} %log_add_fusion, f32[1024]{0:T(1024)S(1)} %bitcast.666), kind=kOutput, calls=%fused_computation.407 | convolution fusion | flops 291900160 | bytes 17576960 | tf_op jit(solution)/shard_map/hqk,hkd->hqd/dot_general | solution.py:226
  1252.5 22.1 %convert_reduce_fusion.29 = (f32[4,64]{1,0:T(4,128)}, bf16[4,512,64]{1,2,0:T(8,128)(2,1)S(1)}) fusion(bf16[4,1024,64]{1,2,0:T(8,128)(2,1)S(1)} %bitcast.561, f32[4,512,1024]{2,1,0:T(8,128)} %fusion.466, f32[4,512,1024]{2,1,0:T(8,128)} %copy-done.1, f32[4,512]{1,0:T(4,128)S(1)} %log_add_fusion.2, f32[1024]{0:T(1024)S(1)} %bitcast.654), kind=kOutput, calls=%fused_computation.408 | convolution fusion | flops 291900160 | bytes 17576960 | tf_op jit(solution)/shard_map/hqk,hkd->hqd/dot_general | solution.py:226
  1337.6 77.7 %reduce-scatter.110.cloned.1.call-done = bf16[2,1024,256]{2,1,0:T(8,128)(2,1)} async-done(((bf16[2,1024,1024]{2,1,0:T(8,128)(2,1)}), bf16[2,1024,256]{2,1,0:T(8,128)(2,1)}) %reduce-scatter.110.cloned.1.call-update) | async-done | bytes 1048592 | tf_op jit(solution)/shard_map/reduce_scatter | solution.py:365
  1415.3 79.5 %reduce-scatter.108.cloned.1.call-done = bf16[2,256,1024]{2,1,0:T(8,128)(2,1)} async-done(((bf16[2,1024,1024]{2,1,0:T(8,128)(2,1)}), bf16[2,256,1024]{2,1,0:T(8,128)(2,1)}) %reduce-scatter.108.cloned.1.call-update) | async-done | bytes 1048592 | tf_op jit(solution)/shard_map/reduce_scatter | solution.py:359
  1494.7 63.2 %reduce-scatter.104.cloned.1.call-done = bf16[2,256,3,256]{3,1,2,0:T(8,128)(2,1)} async-done(((bf16[2,1024,3,256]{3,1,2,0:T(8,128)(2,1)}), bf16[2,256,3,256]{3,1,2,0:T(8,128)(2,1)}) %reduce-scatter.104.cloned.1.call-update) | async-done | bytes 786448 | tf_op jit(solution)/shard_map/reduce_scatter | solution.py:338
  1559.9 19.9 %reduce-scatter.128.cloned.1.call-done = bf16[256,2]{1,0:T(8,128)(2,1)} async-done(((bf16[1024,2]{1,0:T(8,128)(2,1)}), bf16[256,2]{1,0:T(8,128)(2,1)}) %reduce-scatter.128.cloned.1.call-update) | async-done | bytes 1040
  1741.2 22.8 %all-reduce = (f32[2,256]{1,0:T(2,128)}, f32[2,256]{1,0:T(2,128)}, f32[2,256]{1,0:T(2,128)}, f32[2,256]{1,0:T(2,128)}, f32[2,256]{1,0:T(2,128)}, /*index=5*/f32[2,256]{1,0:T(2,128)}) all-reduce(bf16[2,256]{1,0:T(2,128)(2,1)S(1)} %copy.164, bf16[2,256]{1,0:T(2,128)(2,1)S(1)} %copy.166, ...), channel_id=1, replica_groups=mesh['fsdp'=4,'ctx'=2,'tp'=4] {'ctx','tp'}, use_global_device_ids=true, to_apply=%region_73.74 | all-reduce | flops 3072 | bytes 18432 | tf_op jit(solution)/shard_map/psum | solution.py:381
  1764.0 63.7 %all-reduce.5.cloned.1.call-done = (bf16[2,256,3,256]{3,1,2,0:T(8,128)(2,1)}, bf16[2,256,256]{2,1,0:T(8,128)(2,1)}, bf16[2,256,1024]{2,1,0:T(8,128)(2,1)}, bf16[2,1024,256]{2,1,0:T(8,128)(2,1)}) async-done(((bf16[2,256,3,256]{3,1,2,0:T(8,128)(2,1)}, bf16[2,256,256]{2,1,0:T(8,128)(2,1)}, bf16[2,256,1024]{2,1,0:T(8,128)(2,1)}, bf16[2,1024,256]{2,1,0:T(8,128)(2,1)}), (bf16[2,256,3,256]{3,1,2,0:T(8,128)(2,1)}, ...) | async-done | bytes 3145744 | tf_op jit(solution)/shard_map/psum | solution.py:373
  (781 shorter events, 1024.4 us)
Async XLA Ops:
  34.5 112.5 %reduce-scatter.56.cloned.1.call-start = ((), (), s32[]{:S(2)}) async-start(), calls=%async_computation.38 | async-start | bytes 1310720 | tf_op jit(solution)/shard_map/reduce_scatter | solution.py:57
  225.7 127.9 %all-gather.87.cloned.1.call-start = ((), (), s32[]{:S(2)}) async-start(), calls=%async_computation.81 | async-start | bytes 2621440 | tf_op jit(solution)/shard_map/all_gather | solution.py:96
  226.9 161.3 %reduce-scatter.58.cloned.1.call-start = ((), (), s32[]{:S(2)}) async-start(), calls=%async_computation.40 | async-start | bytes 1310720 | tf_op jit(solution)/shard_map/reduce_scatter | solution.py:57
  362.7 110.7 %all-gather.67.cloned.1.call-start = ((), (), s32[]{:S(2)}) async-start(), calls=%async_computation.49 | async-start | bytes 1310720 | tf_op jit(solution)/shard_map/all_gather | solution.py:49
  411.8 164.8 %reduce-scatter.68.cloned.1.call-start = ((), (), s32[]{:S(2)}) async-start(), calls=%async_computation.50 | async-start | bytes 1310720 | tf_op jit(solution)/shard_map/reduce_scatter | solution.py:57
  582.1 145.1 %all-gather.93.cloned.1.call-start = ((), (), s32[]{:S(2)}) async-start(), calls=%async_computation.84 | async-start | bytes 2621440 | tf_op jit(solution)/shard_map/all_gather | solution.py:96
  582.8 160.9 %all-gather.95.cloned.1.call-start = ((), (), s32[]{:S(2)}) async-start(), calls=%async_computation.85 | async-start | bytes 1310720 | tf_op jit(solution)/shard_map/all_gather | solution.py:53
  583.6 188.3 %reduce-scatter.88.cloned.1.call-start = ((), (), s32[]{:S(2)}) async-start(), calls=%async_computation.64 | async-start | bytes 1310720 | tf_op jit(solution)/shard_map/reduce_scatter | solution.py:63
  760.9 113.2 %all-gather.77.cloned.1.call-start = ((), (), s32[]{:S(2)}) async-start(), calls=%async_computation.65 | async-start | bytes 1310720 | tf_op jit(solution)/shard_map/all_gather | solution.py:53
  858.0 115.2 %reduce-scatter.90.cloned.1.call-start = ((), (), s32[]{:S(2)}) async-start(), calls=%async_computation.66 | async-start | bytes 786432 | tf_op jit(solution)/shard_map/reduce_scatter | solution.py:232
  1135.2 113.6 %reduce-scatter.98.cloned.1.call-start = ((), (), s32[]{:S(2)}) async-start(), calls=%async_computation.72 | async-start | bytes 786432 | tf_op jit(solution)/shard_map/reduce_scatter | solution.py:232
  1283.2 132.0 %reduce-scatter.110.cloned.1.call-start = ((), (), s32[]{:S(2)}) async-start(), calls=%async_computation.78 | async-start | bytes 5242880 | tf_op jit(solution)/shard_map/reduce_scatter | solution.py:365
  1293.4 201.3 %reduce-scatter.108.cloned.1.call-start = ((), (), s32[]{:S(2)}) async-start(), calls=%async_computation.77 | async-start | bytes 5242880 | tf_op jit(solution)/shard_map/reduce_scatter | solution.py:359
  1303.4 254.6 %reduce-scatter.104.cloned.1.call-start = ((), (), s32[]{:S(2)}) async-start(), calls=%async_computation.75 | async-start | bytes 3932160 | tf_op jit(solution)/shard_map/reduce_scatter | solution.py:338
  1312.7 267.0 %reduce-scatter.128.cloned.1.call-start = ((), (), s32[]{:S(2)}) async-start(), calls=%async_computation.95 | async-start | bytes 327680
  1314.8 284.5 %reduce-scatter.126.cloned.1.call-start = ((), (), s32[]{:S(2)}) async-start(), calls=%async_computation.94 | async-start | bytes 20480
  1315.8 303.4 %reduce-scatter.124.cloned.1.call-start = ((), (), s32[]{:S(2)}) async-start(), calls=%async_computation.93 | async-start | bytes 327680
  1316.8 322.7 %reduce-scatter.122.cloned.1.call-start = ((), (), s32[]{:S(2)}) async-start(), calls=%async_computation.92 | async-start | bytes 327680
  1317.8 341.9 %reduce-scatter.120.cloned.1.call-start = ((), (), s32[]{:S(2)}) async-start(), calls=%async_computation.91 | async-start | bytes 327680
  1318.7 361.0 %reduce-scatter.116.cloned.1.call-start = ((), (), s32[]{:S(2)}) async-start(), calls=%async_computation.89 | async-start | bytes 20480
  1319.7 379.4 %reduce-scatter.118.cloned.1.call-start = ((), (), s32[]{:S(2)}) async-start(), calls=%async_computation.90 | async-start | bytes 20480
  1320.9 398.8 %reduce-scatter.114.cloned.1.call-start = ((), (), s32[]{:S(2)}) async-start(), calls=%async_computation.88 | async-start | bytes 327680
  1325.1 415.2 %reduce-scatter.112.cloned.1.call-start = ((), (), s32[]{:S(2)}) async-start(), calls=%async_computation.87 | async-start | bytes 327680
  1326.1 501.6 %all-reduce.5.cloned.1.call-start = ((), (), s32[]{:S(2)}) async-start(), calls=%async_computation.96 | async-start | bytes 6291456 | tf_op jit(solution)/shard_map/psum | solution.py:373
  (186 other events, 5320.8 us)
Sparse Core Ops, SparseCore 0:
  52.1 41.7 all-gather.82
  121.3 25.6 reduce-scatter.55
  195.5 24.8 reduce-scatter.63
  222.4 46.2 all-gather.84
  307.4 46.2 all-gather.86
  410.3 44.1 all-gather.88
  523.5 24.8 reduce-scatter.67
  551.5 24.9 reduce-scatter.59
  578.5 46.1 all-gather.90
  680.9 46.2 all-gather.92
  746.3 24.8 reduce-scatter.87
  773.7 24.8 reduce-scatter.71
  801.2 24.9 reduce-scatter.61
  828.7 24.8 reduce-scatter.69
  979.3 25.0 reduce-scatter.93
  1007.1 24.8 reduce-scatter.77
  1074.9 24.8 reduce-scatter.95
  1103.1 24.9 reduce-scatter.79
  1283.3 24.9 reduce-scatter.85
  1310.4 27.1 reduce-scatter.105
  1339.8 75.4 reduce-scatter.109
  1417.4 77.2 reduce-scatter.107
  1497.1 60.7 reduce-scatter.103
  1742.7 84.8 all-reduce.4
  (36 shorter events, 610.7 us)
where the time goes:
time: 1850 us; the launch traced here: 1840 us
  waiting for transfers between devices  986 us (53%)
  matrix products  382 us (21%)
  blocking collectives  331 us (18%)
  other arithmetic  66.7 us (4%)
  local copies, waits for them, and re-layouts  54.1 us (3%)
    unnamed x69, waiting for transfers between devices  168 us
    all_gather x8, waiting for transfers between devices, spread_rows(): return lax.all_gather(rows, 'tp', axis=0, tiled=True)  106 us
    reduce_scatter x8, waiting for transfers between devices, combine_grads(): lax.psum_scatter(partial_value.astype(jnp.bfloat16), 'tp', scatter_dimens...  103 us
    reduce_scatter x8, waiting for transfers between devices, combine_rows(): lax.psum_scatter(partial_value.astype(jnp.bfloat16), 'tp', scatter_dimens...  92.7 us
    dot_general x4, matrix products, backward_layer(): jnp.einsum('hqk,hqd->hkd', d_raw, query_heads, preferred_element_type=jnp...  89.9 us
    dot_general x4, matrix products, backward_layer(): jnp.einsum('hqk,hkd->hqd', d_raw, key_heads, preferred_element_type=jnp.f...  87.6 us
    all_gather x2, waiting for transfers between devices, fetch(): lax.all_gather(reduce_weight[layer_id], 'fsdp', axis=1, tiled=True)  83.4 us
    reduce_scatter x1, waiting for transfers between devices, local(): lax.psum_scatter(stacked[9].astype(jnp.bfloat16), 'fsdp', scatter_dimensi...  79.5 us
  transfers between devices with their start and end apart: 60, of which 42 were waited for; matrix products, arithmetic and copies ran while one was open for 23% of the time, Pallas kernels for 0%

commit v1 on v0

--- a/solution.py
+++ b/solution.py
@@ -370,7 +370,9 @@
         ).astype(jnp.float32),
     )
     split_sums = (
-        lax.psum(shards[2].astype(jnp.bfloat16), "ctx").astype(jnp.float32),
+        jnp.sum(jax.lax.all_gather(shards[2].astype(jnp.bfloat16), axis_name="ctx"), axis=0).astype(
+            jnp.float32
+        ),
         lax.psum(shards[3].astype(jnp.bfloat16), "ctx").astype(jnp.float32),
         lax.psum(shards[4].astype(jnp.bfloat16), "ctx").astype(jnp.float32),
         lax.psum(shards[5].astype(jnp.bfloat16), "ctx").astype(jnp.float32),

time: 1850 us -> 1860 us (level)
    all_gather x0 -> x1, waiting for transfers between devices: none -> 23.7 us  [local(): jax.lax.all_gather(shards[2].astype(jnp.bfloat16), axis_name='ctx')]
    unnamed x69 -> x70, waiting for transfers between devices: 168 us -> 168 us
  transfers between devices with their start and end apart: 60 -> 61, of which waited for: 42 -> 43; matrix products, arithmetic and copies ran while one was open for 23% -> 23% of each run, Pallas kernels for 0% -> 0%
where the time goes in v1:
time: 1860 us; the launch traced here: 1850 us
  waiting for transfers between devices  990 us (53%)
  matrix products  380 us (20%)
  blocking collectives  331 us (18%)
  other arithmetic  68.3 us (4%)
  local copies, waits for them, and re-layouts  54.3 us (3%)
    unnamed x70, waiting for transfers between devices  168 us
    all_gather x8, waiting for transfers between devices, spread_rows(): return lax.all_gather(rows, 'tp', axis=0, tiled=True)  106 us
    reduce_scatter x8, waiting for transfers between devices, combine_grads(): lax.psum_scatter(partial_value.astype(jnp.bfloat16), 'tp', scatter_dimens...  103 us
    reduce_scatter x8, waiting for transfers between devices, combine_rows(): lax.psum_scatter(partial_value.astype(jnp.bfloat16), 'tp', scatter_dimens...  92.6 us
    dot_general x4, matrix products, backward_layer(): jnp.einsum('hqk,hqd->hkd', d_raw, query_heads, preferred_element_type=jnp...  90.6 us
    dot_general x4, matrix products, backward_layer(): jnp.einsum('hqk,hkd->hqd', d_raw, key_heads, preferred_element_type=jnp.f...  86.4 us
    all_gather x2, waiting for transfers between devices, fetch(): lax.all_gather(reduce_weight[layer_id], 'fsdp', axis=1, tiled=True)  83.4 us
    reduce_scatter x1, waiting for transfers between devices, local(): lax.psum_scatter(stacked[9].astype(jnp.bfloat16), 'fsdp', scatter_dimensi...  79.5 us
  transfers between devices with their start and end apart: 61, of which 43 were waited for; matrix products, arithmetic and copies ran while one was open for 23% of the time, Pallas kernels for 0%

profile of v1, /device:TPU:0, one launch (start us, length us, event | category | flops | bytes accessed | tf_op | source)
XLA Modules:
  0.0 1846.4 jit_solution(11932278154673312541)
XLA Ops:
  240.8 27.9 %all-gather.87.cloned.1.call-done = bf16[1,1024,1024]{2,1,0:T(8,128)(2,1)} async-done(((bf16[1,256,1024]{2,1,0:T(8,128)(2,1)}), bf16[1,1024,1024]{2,1,0:T(8,128)(2,1)}) %all-gather.87.cloned.1.call-update) | async-done | bytes 2097168 | tf_op jit(solution)/shard_map/all_gather | solution.py:94
  318.6 35.0 %all-gather.89.cloned.1.call-done = bf16[1,1024,1024]{2,1,0:T(8,128)(2,1)} async-done(((bf16[1,1024,256]{2,1,0:T(8,128)(2,1)}), bf16[1,1024,1024]{2,1,0:T(8,128)(2,1)}) %all-gather.89.cloned.1.call-update) | async-done | bytes 2097168 | tf_op jit(solution)/shard_map/all_gather | solution.py:96
  388.2 20.1 %reduce-scatter.66.cloned.1.call-done = bf16[128,1024]{1,0:T(8,128)(2,1)} async-done(((bf16[512,1024]{1,0:T(8,128)(2,1)}), bf16[128,1024]{1,0:T(8,128)(2,1)}) %reduce-scatter.66.cloned.1.call-update) | async-done | bytes 262160 | tf_op jit(solution)/shard_map/reduce_scatter | solution.py:57
  597.3 27.4 %all-gather.93.cloned.1.call-done = bf16[1,1024,1024]{2,1,0:T(8,128)(2,1)} async-done(((bf16[1,256,1024]{2,1,0:T(8,128)(2,1)}), bf16[1,1024,1024]{2,1,0:T(8,128)(2,1)}) %all-gather.93.cloned.1.call-update) | async-done | bytes 2097168 | tf_op jit(solution)/shard_map/all_gather | solution.py:94
  678.8 48.4 %all-gather.95.cloned.1.call-done = bf16[1,1024,1024]{2,1,0:T(8,128)(2,1)} async-done(((bf16[1,1024,256]{2,1,0:T(8,128)(2,1)}), bf16[1,1024,1024]{2,1,0:T(8,128)(2,1)}) %all-gather.95.cloned.1.call-update) | async-done | bytes 2097168 | tf_op jit(solution)/shard_map/all_gather | solution.py:96
  771.9 26.8 %reduce-scatter.72.cloned.1.call-done = bf16[128,1024]{1,0:T(8,128)(2,1)} async-done(((bf16[512,1024]{1,0:T(8,128)(2,1)}), bf16[128,1024]{1,0:T(8,128)(2,1)}) %reduce-scatter.72.cloned.1.call-update) | async-done | bytes 262160 | tf_op jit(solution)/shard_map/reduce_scatter | solution.py:63
  800.2 26.0 %reduce-scatter.62.cloned.1.call-done = bf16[128,1024]{1,0:T(8,128)(2,1)} async-done(((bf16[512,1024]{1,0:T(8,128)(2,1)}), bf16[128,1024]{1,0:T(8,128)(2,1)}) %reduce-scatter.62.cloned.1.call-update) | async-done | bytes 262160 | tf_op jit(solution)/shard_map/reduce_scatter | solution.py:57
  826.1 27.5 %reduce-scatter.70.cloned.1.call-done = bf16[128,1024]{1,0:T(8,128)(2,1)} async-done(((bf16[512,1024]{1,0:T(8,128)(2,1)}), bf16[128,1024]{1,0:T(8,128)(2,1)}) %reduce-scatter.70.cloned.1.call-update) | async-done | bytes 262160 | tf_op jit(solution)/shard_map/reduce_scatter | solution.py:57
  881.5 22.9 %fusion.221 = bf16[4,1024,64]{1,2,0:T(8,128)(2,1)} fusion(f32[4,512,1024]{2,1,0:T(8,128)} %fusion.467, f32[4,512,1024]{2,1,0:T(8,128)} %copy-done.4, f32[4,512]{1,0:T(4,128)S(1)} %log_add_fusion.1, f32[1024]{0:T(1024)S(1)} %bitcast.663, f32[512,4,64]{0,2,1:T(8,128)S(1)} %bitcast.580, f32[4,64]{1,0:T(4,128)S(1)} %copy.126), kind=kOutput, calls=%fused_computation.234 | convolution fusion | flops 292031488 | bytes 17839104 | tf_op jit(solution)/shard_map/hqk,hqd->hkd/dot_general | solution.py:228
  921.4 22.0 %fusion.227 = bf16[4,1024,64]{1,2,0:T(8,128)(2,1)S(1)} fusion(f32[4,512,1024]{2,1,0:T(8,128)} %fusion.465, f32[4,512,1024]{2,1,0:T(8,128)} %copy-done.3, f32[4,512]{1,0:T(4,128)S(1)} %log_add_fusion.3, f32[1024]{0:T(1024)S(1)} %bitcast.651, f32[512,4,64]{0,2,1:T(8,128)S(1)} %bitcast.578, f32[4,64]{1,0:T(4,128)S(1)} %copy.126), kind=kOutput, calls=%fused_computation.236 | convolution fusion | flops 292031488 | bytes 17839104 | tf_op jit(solution)/shard_map/hqk,hqd->hkd/dot_general | solution.py:228
  951.1 21.7 %convert_reduce_fusion.26 = (f32[4,64]{1,0:T(4,128)S(1)}, bf16[4,512,64]{1,2,0:T(8,128)(2,1)S(1)}) fusion(bf16[4,1024,64]{1,2,0:T(8,128)(2,1)S(1)} %bitcast.576, f32[4,512,1024]{2,1,0:T(8,128)} %fusion.467, f32[4,512,1024]{2,1,0:T(8,128)} %copy-done.4, f32[4,512]{1,0:T(4,128)S(1)} %log_add_fusion.1, f32[1024]{0:T(1024)S(1)} %bitcast.665), kind=kOutput, calls=%fused_computation.405 | convolution fusion | flops 291900160 | bytes 17576960 | tf_op jit(solution)/shard_map/hqk,hkd->hqd/dot_general | solution.py:226
  976.8 21.5 %convert_reduce_fusion.27 = (f32[4,64]{1,0:T(4,128)S(1)}, bf16[4,512,64]{1,2,0:T(8,128)(2,1)S(1)}) fusion(bf16[4,1024,64]{1,2,0:T(8,128)(2,1)S(1)} %bitcast.574, f32[4,512,1024]{2,1,0:T(8,128)} %fusion.465, f32[4,512,1024]{2,1,0:T(8,128)} %copy-done.3, f32[4,512]{1,0:T(4,128)S(1)} %log_add_fusion.3, f32[1024]{0:T(1024)S(1)} %bitcast.653), kind=kOutput, calls=%fused_computation.406 | convolution fusion | flops 291900160 | bytes 17576960 | tf_op jit(solution)/shard_map/hqk,hkd->hqd/dot_general | solution.py:226
  1004.3 27.5 %reduce-scatter.78.cloned.1.call-done = bf16[128,1024]{1,0:T(8,128)(2,1)} async-done(((bf16[512,1024]{1,0:T(8,128)(2,1)}), bf16[128,1024]{1,0:T(8,128)(2,1)}) %reduce-scatter.78.cloned.1.call-update) | async-done | bytes 262160 | tf_op jit(solution)/shard_map/reduce_scatter | solution.py:63
  1099.7 28.2 %reduce-scatter.80.cloned.1.call-done = bf16[128,1024]{1,0:T(8,128)(2,1)} async-done(((bf16[512,1024]{1,0:T(8,128)(2,1)}), bf16[128,1024]{1,0:T(8,128)(2,1)}) %reduce-scatter.80.cloned.1.call-update) | async-done | bytes 262160 | tf_op jit(solution)/shard_map/reduce_scatter | solution.py:63
  1164.0 22.8 %fusion.218 = bf16[4,1024,64]{1,2,0:T(8,128)(2,1)} fusion(f32[4,512,1024]{2,1,0:T(8,128)} %fusion.468, f32[4,512,1024]{2,1,0:T(8,128)} %copy-done.2, f32[4,512]{1,0:T(4,128)S(1)} %log_add_fusion, f32[1024]{0:T(1024)S(1)} %bitcast.667, f32[512,4,64]{0,2,1:T(8,128)S(1)} %bitcast.570, f32[4,64]{1,0:T(4,128)S(1)} %copy-done.103), kind=kOutput, calls=%fused_computation.233 | convolution fusion | flops 292031488 | bytes 17839104 | tf_op jit(solution)/shard_map/hqk,hqd->hkd/dot_general | solution.py:228
  1201.6 22.8 %fusion.224 = bf16[4,1024,64]{1,2,0:T(8,128)(2,1)} fusion(f32[4,512,1024]{2,1,0:T(8,128)} %fusion.466, f32[4,512,1024]{2,1,0:T(8,128)} %copy-done.1, f32[4,512]{1,0:T(4,128)S(1)} %log_add_fusion.2, f32[1024]{0:T(1024)S(1)} %bitcast.655, f32[512,4,64]{0,2,1:T(8,128)S(1)} %bitcast.564, f32[4,64]{1,0:T(4,128)S(1)} %copy-done.103), kind=kOutput, calls=%fused_computation.235 | convolution fusion | flops 292031488 | bytes 17839104 | tf_op jit(solution)/shard_map/hqk,hqd->hkd/dot_general | solution.py:228
  1226.7 21.6 %convert_reduce_fusion.28 = (f32[4,64]{1,0:T(4,128)S(1)}, bf16[4,512,64]{1,2,0:T(8,128)(2,1)S(1)}) fusion(bf16[4,1024,64]{1,2,0:T(8,128)(2,1)S(1)} %bitcast.568, f32[4,512,1024]{2,1,0:T(8,128)} %fusion.468, f32[4,512,1024]{2,1,0:T(8,128)} %copy-done.2, f32[4,512]{1,0:T(4,128)S(1)} %log_add_fusion, f32[1024]{0:T(1024)S(1)} %bitcast.668), kind=kOutput, calls=%fused_computation.407 | convolution fusion | flops 291900160 | bytes 17576960 | tf_op jit(solution)/shard_map/hqk,hkd->hqd/dot_general | solution.py:226
  1252.1 21.6 %convert_reduce_fusion.29 = (f32[4,64]{1,0:T(4,128)S(1)}, bf16[4,512,64]{1,2,0:T(8,128)(2,1)S(1)}) fusion(bf16[4,1024,64]{1,2,0:T(8,128)(2,1)S(1)} %bitcast.562, f32[4,512,1024]{2,1,0:T(8,128)} %fusion.466, f32[4,512,1024]{2,1,0:T(8,128)} %copy-done.1, f32[4,512]{1,0:T(4,128)S(1)} %log_add_fusion.2, f32[1024]{0:T(1024)S(1)} %bitcast.656), kind=kOutput, calls=%fused_computation.408 | convolution fusion | flops 291900160 | bytes 17576960 | tf_op jit(solution)/shard_map/hqk,hkd->hqd/dot_general | solution.py:226
  1334.6 77.7 %reduce-scatter.110.cloned.1.call-done = bf16[2,1024,256]{2,1,0:T(8,128)(2,1)} async-done(((bf16[2,1024,1024]{2,1,0:T(8,128)(2,1)}), bf16[2,1024,256]{2,1,0:T(8,128)(2,1)}) %reduce-scatter.110.cloned.1.call-update) | async-done | bytes 1048592 | tf_op jit(solution)/shard_map/reduce_scatter | solution.py:365
  1412.3 79.5 %reduce-scatter.108.cloned.1.call-done = bf16[2,256,1024]{2,1,0:T(8,128)(2,1)} async-done(((bf16[2,1024,1024]{2,1,0:T(8,128)(2,1)}), bf16[2,256,1024]{2,1,0:T(8,128)(2,1)}) %reduce-scatter.108.cloned.1.call-update) | async-done | bytes 1048592 | tf_op jit(solution)/shard_map/reduce_scatter | solution.py:359
  1491.8 63.1 %reduce-scatter.104.cloned.1.call-done = bf16[2,256,3,256]{3,1,2,0:T(8,128)(2,1)} async-done(((bf16[2,1024,3,256]{3,1,2,0:T(8,128)(2,1)}), bf16[2,256,3,256]{3,1,2,0:T(8,128)(2,1)}) %reduce-scatter.104.cloned.1.call-update) | async-done | bytes 786448 | tf_op jit(solution)/shard_map/reduce_scatter | solution.py:338
  1738.2 22.8 %all-reduce = (f32[2,256]{1,0:T(2,128)}, f32[2,256]{1,0:T(2,128)}, f32[2,256]{1,0:T(2,128)}, f32[2,256]{1,0:T(2,128)}, f32[2,256]{1,0:T(2,128)}, /*index=5*/f32[2,256]{1,0:T(2,128)}) all-reduce(bf16[2,256]{1,0:T(2,128)(2,1)S(1)} %copy.164, bf16[2,256]{1,0:T(2,128)(2,1)S(1)} %copy.166, ...), channel_id=1, replica_groups=mesh['fsdp'=4,'ctx'=2,'tp'=4] {'ctx','tp'}, use_global_device_ids=true, to_apply=%region_73.74 | all-reduce | flops 3072 | bytes 18432 | tf_op jit(solution)/shard_map/psum | solution.py:383
  1761.0 46.3 %all-reduce.5.cloned.1.call-done = (bf16[2,256,256]{2,1,0:T(8,128)(2,1)}, bf16[2,256,1024]{2,1,0:T(8,128)(2,1)}, bf16[2,1024,256]{2,1,0:T(8,128)(2,1)}) async-done(((bf16[2,256,256]{2,1,0:T(8,128)(2,1)}, bf16[2,256,1024]{2,1,0:T(8,128)(2,1)}, bf16[2,1024,256]{2,1,0:T(8,128)(2,1)}), (bf16[2,256,256]{2,1,0:T(8,128)(2,1)}, bf16[2,256,1024]{2,1,0:T(8,128)(2,1)}, ...) | async-done | bytes 2359312 | tf_op jit(solution)/shard_map/psum | solution.py:378
  1812.4 23.7 %all-gather.101.cloned.1.call-done = bf16[4,256,3,256]{3,1,2,0:T(8,128)(2,1)} async-done(((bf16[2,256,3,256]{3,1,2,0:T(8,128)(2,1)}), bf16[4,256,3,256]{3,1,2,0:T(8,128)(2,1)}) %all-gather.101.cloned.1.call-update) | async-done | bytes 1572880 | tf_op jit(solution)/shard_map/all_gather | solution.py:373
  (779 shorter events, 1043.9 us)
Async XLA Ops:
  34.5 112.5 %reduce-scatter.56.cloned.1.call-start = ((), (), s32[]{:S(2)}) async-start(), calls=%async_computation.38 | async-start | bytes 1310720 | tf_op jit(solution)/shard_map/reduce_scatter | solution.py:57
  225.7 127.9 %all-gather.89.cloned.1.call-start = ((), (), s32[]{:S(2)}) async-start(), calls=%async_computation.81 | async-start | bytes 2621440 | tf_op jit(solution)/shard_map/all_gather | solution.py:96
  226.9 161.3 %reduce-scatter.58.cloned.1.call-start = ((), (), s32[]{:S(2)}) async-start(), calls=%async_computation.40 | async-start | bytes 1310720 | tf_op jit(solution)/shard_map/reduce_scatter | solution.py:57
  411.8 164.8 %reduce-scatter.68.cloned.1.call-start = ((), (), s32[]{:S(2)}) async-start(), calls=%async_computation.50 | async-start | bytes 1310720 | tf_op jit(solution)/shard_map/reduce_scatter | solution.py:57
  582.1 145.1 %all-gather.95.cloned.1.call-start = ((), (), s32[]{:S(2)}) async-start(), calls=%async_computation.84 | async-start | bytes 2621440 | tf_op jit(solution)/shard_map/all_gather | solution.py:96
  582.8 160.9 %all-gather.97.cloned.1.call-start = ((), (), s32[]{:S(2)}) async-start(), calls=%async_computation.85 | async-start | bytes 1310720 | tf_op jit(solution)/shard_map/all_gather | solution.py:53
  583.6 188.4 %reduce-scatter.88.cloned.1.call-start = ((), (), s32[]{:S(2)}) async-start(), calls=%async_computation.64 | async-start | bytes 1310720 | tf_op jit(solution)/shard_map/reduce_scatter | solution.py:63
  761.0 113.2 %all-gather.79.cloned.1.call-start = ((), (), s32[]{:S(2)}) async-start(), calls=%async_computation.65 | async-start | bytes 1310720 | tf_op jit(solution)/shard_map/all_gather | solution.py:53
  858.0 115.0 %reduce-scatter.90.cloned.1.call-start = ((), (), s32[]{:S(2)}) async-start(), calls=%async_computation.66 | async-start | bytes 786432 | tf_op jit(solution)/shard_map/reduce_scatter | solution.py:232
  1135.0 113.4 %reduce-scatter.100.cloned.1.call-start = ((), (), s32[]{:S(2)}) async-start(), calls=%async_computation.73 | async-start | bytes 786432 | tf_op jit(solution)/shard_map/reduce_scatter | solution.py:235
  1282.4 129.9 %reduce-scatter.110.cloned.1.call-start = ((), (), s32[]{:S(2)}) async-start(), calls=%async_computation.78 | async-start | bytes 5242880 | tf_op jit(solution)/shard_map/reduce_scatter | solution.py:365
  1292.6 199.1 %reduce-scatter.108.cloned.1.call-start = ((), (), s32[]{:S(2)}) async-start(), calls=%async_computation.77 | async-start | bytes 5242880 | tf_op jit(solution)/shard_map/reduce_scatter | solution.py:359
  1302.7 252.2 %reduce-scatter.104.cloned.1.call-start = ((), (), s32[]{:S(2)}) async-start(), calls=%async_computation.75 | async-start | bytes 3932160 | tf_op jit(solution)/shard_map/reduce_scatter | solution.py:338
  1312.1 264.8 %reduce-scatter.128.cloned.1.call-start = ((), (), s32[]{:S(2)}) async-start(), calls=%async_computation.96 | async-start | bytes 327680
  1314.1 282.1 %reduce-scatter.126.cloned.1.call-start = ((), (), s32[]{:S(2)}) async-start(), calls=%async_computation.95 | async-start | bytes 20480
  1315.1 301.1 %reduce-scatter.124.cloned.1.call-start = ((), (), s32[]{:S(2)}) async-start(), calls=%async_computation.94 | async-start | bytes 327680
  1316.1 320.3 %reduce-scatter.122.cloned.1.call-start = ((), (), s32[]{:S(2)}) async-start(), calls=%async_computation.93 | async-start | bytes 327680
  1317.1 339.6 %reduce-scatter.120.cloned.1.call-start = ((), (), s32[]{:S(2)}) async-start(), calls=%async_computation.92 | async-start | bytes 327680
  1318.1 358.6 %reduce-scatter.116.cloned.1.call-start = ((), (), s32[]{:S(2)}) async-start(), calls=%async_computation.90 | async-start | bytes 20480
  1319.0 377.0 %reduce-scatter.118.cloned.1.call-start = ((), (), s32[]{:S(2)}) async-start(), calls=%async_computation.91 | async-start | bytes 20480
  1320.2 396.4 %reduce-scatter.114.cloned.1.call-start = ((), (), s32[]{:S(2)}) async-start(), calls=%async_computation.89 | async-start | bytes 327680
  1324.4 412.9 %reduce-scatter.112.cloned.1.call-start = ((), (), s32[]{:S(2)}) async-start(), calls=%async_computation.88 | async-start | bytes 327680
  1325.4 481.8 %all-reduce.5.cloned.1.call-start = ((), (), s32[]{:S(2)}) async-start(), calls=%async_computation.97 | async-start | bytes 4718592 | tf_op jit(solution)/shard_map/psum | solution.py:378
  1491.8 344.3 %all-gather.101.cloned.1.call-start = ((), (), s32[]{:S(2)}) async-start(), calls=%async_computation.87 | async-start | bytes 2359296 | tf_op jit(solution)/shard_map/all_gather | solution.py:373
  (184 other events, 5763.1 us)
Sparse Core Ops, SparseCore 0:
  52.1 41.7 all-gather.84
  121.3 25.6 reduce-scatter.55
  195.5 24.8 reduce-scatter.63
  222.4 46.2 all-gather.86
  307.4 46.2 all-gather.88
  410.3 44.1 all-gather.90
  551.5 24.9 reduce-scatter.59
  578.5 46.1 all-gather.92
  680.9 46.2 all-gather.94
  746.3 24.8 reduce-scatter.87
  773.8 24.8 reduce-scatter.71
  801.2 24.8 reduce-scatter.61
  828.7 24.8 reduce-scatter.69
  979.1 25.1 reduce-scatter.93
  1074.7 24.8 reduce-scatter.95
  1102.9 24.8 reduce-scatter.79
  1252.2 24.9 reduce-scatter.101
  1280.3 24.9 reduce-scatter.85
  1307.4 27.1 reduce-scatter.105
  1336.8 75.4 reduce-scatter.109
  1414.4 77.2 reduce-scatter.107
  1494.1 60.7 reduce-scatter.103
  1739.7 67.4 all-reduce.4
  1808.9 27.2 all-gather.100
  (37 shorter events, 635.3 us)
